TPU v7x, 32 devices: a whole 2x2x4 slice. The times are simulated.
32 devices in a mesh: prow: 4 (over y, x), pcol: 8 (over z, core).
Axes of the slice: x: 2, y: 2, z: 4, core: 2. Of those that a mesh axis runs over, the one named last changes fastest.
Arguments:
- ancestor: float32 [12288, 12288], P('prow', 'pcol'), may hold values from -448 to 15360, as said below
- factor: bfloat16 [2, 12288, 256], P(None, 'prow'), may hold values from -0.0009765625 to 0.0009765625
- inverse_diag: bfloat16 [2, 256, 256], replicated, may hold values from -6 to 6
- block_mask: int32 [2, 48], replicated, may hold values 0 or 1
Outputs:
- column_block: float32 [2, 12288, 256], P(None, ('prow', 'pcol'))
- diagonal: float32 [2, 256, 256], replicated
Inputs may be any that keep to these rules, and one draw needn't show every extreme that they name: `ancestor`: symmetric.
All inputs are finite; a program needn't handle non-finite values.
Results may differ from a plain program's by a relative error of at most 0.0003.
Values may be sent and summed in bfloat16 or wider, within the bound.
A program may use at most 64 MiB of HBM per device.

v0:
```python
import jax
import jax.numpy as jnp
from jax import lax
from jax.sharding import PartitionSpec as P

WIDTH = 256


def broadcast(shard, axis, root):
    mine = lax.axis_index(axis) == root
    return lax.psum(jnp.where(mine, shard, jnp.zeros_like(shard)), axis)


def multiply(ancestor, received, col_mask, own_mask):
    weighted = received.astype(jnp.float32) * col_mask[:, :, None]
    product = jnp.einsum(
        "ij,kjw->kiw",
        ancestor,
        weighted,
        precision=lax.Precision.HIGHEST,
        preferred_element_type=jnp.float32,
    )
    return -own_mask[:, :, None] * product


def reduced_term(own_rows, column_block, column):
    slab = column_block.shape[1]
    own_slab = lax.dynamic_slice_in_dim(own_rows, column * slab, slab, 1)
    return jnp.einsum(
        "kiw,kiv->kwv",
        own_slab,
        column_block,
        precision=lax.Precision.HIGHEST,
        preferred_element_type=jnp.float32,
    )


def shards(ancestor, factor, inverse_diag, block_mask):
    rows_here = ancestor.shape[0]
    cols_here = ancestor.shape[1]
    n_rows = lax.axis_size("prow")
    n_cols = lax.axis_size("pcol")
    per_row = n_cols // n_rows
    column = lax.axis_index("pcol")
    grid_row = lax.axis_index("prow")
    root_row = column // per_row
    offset = column % per_row * cols_here
    row_mask = jnp.repeat(block_mask, WIDTH, axis=1).astype(jnp.float32)
    own_mask = lax.dynamic_slice_in_dim(row_mask, grid_row * rows_here, rows_here, 1)
    col_mask = lax.dynamic_slice_in_dim(row_mask, column * cols_here, cols_here, 1)
    own_rows = factor.astype(jnp.float32) * own_mask[:, :, None]
    col_part = lax.dynamic_slice_in_dim(factor, offset, cols_here, 1)
    pieces = []
    blocks = []
    for supernode in range(factor.shape[0]):
        received = broadcast(col_part[supernode : supernode + 1], "prow", root_row)
        negated_one = multiply(
            ancestor,
            received,
            col_mask[supernode : supernode + 1],
            own_mask[supernode : supernode + 1],
        )
        blocks.append(lax.psum_scatter(negated_one, "pcol", scatter_dimension=1, tiled=True))
        pieces.append(negated_one)
    column_block = jnp.concatenate(blocks, 0)
    term = reduced_term(own_rows, column_block, column)
    total = lax.psum(term, ("prow", "pcol"))
    diagonal = inverse_diag.astype(jnp.float32) - total
    return (column_block, diagonal)


def solution(mesh):
    return jax.shard_map(
        shards,
        mesh=mesh,
        in_specs=(P("prow", "pcol"), P(None, "prow", None), P(), P()),
        out_specs=(P(None, ("prow", "pcol"), None), P()),
        check_vma=False,
    )
```

profile of v0, /device:TPU:0, one launch (start us, length us, event | category | flops | bytes accessed | tf_op | source)
XLA Modules:
  0.0 335.2 jit_solution(11929056268012232022)
XLA Ops:
  7.2 0.0 copy-start.2
  7.2 0.0 all-reduce.6.cloned.1.call-start
  7.2 2.8 dynamic-slice_select_fusion
  10.1 0.0 all-reduce.6.cloned.1.call-update
  10.1 0.0 reduce-scatter.3.cloned.1.call-start
  10.1 0.0 copy-done.2
  10.2 0.1 broadcast_bitcast_fusion
  10.2 0.1 copy.11
  10.3 0.1 dynamic-slice_reduce_fusion
  10.4 0.1 dynamic-slice_negate_fusion
  10.5 64.6 %all-reduce.6.cloned.1.call-done = (bf16[1,1536,256]{2,1,0:T(8,128)(2,1)}, bf16[1,1536,256]{2,1,0:T(8,128)(2,1)}) async-done(((bf16[1,1536,256]{2,1,0:T(8,128)(2,1)}, bf16[1,1536,256]{2,1,0:T(8,128)(2,1)}), (bf16[1,1536,256]{2,1,0:T(8,128)(2,1)}, bf16[1,1536,256]{2,1,0:T(8,128)(2,1)})) %all-reduce.6.cloned.1.call-update) | async-done | bytes 1572880 | tf_op jit(solution)/shard_map/psum | solution.py:11
  75.2 35.3 %fusion.3 = f32[1,3072,256]{1,2,0:T(8,128)} fusion(f32[3072,1536]{1,0:T(8,128)} %param.4, bf16[1,1536,256]{2,1,0:T(8,128)(2,1)} %get-tuple-element.6, f32[3072]{0:T(1024)S(1)} %bitcast.34, f32[1536]{0:T(1024)S(1)} %get-tuple-element.5), kind=kOutput, calls=%fused_computation.5 | convolution fusion | flops 14497087488 | bytes 22824960 | tf_op jit(solution)/shard_map/ij,kjw->kiw/dot_general | solution.py:16
  110.4 0.0 copy-start
  110.4 0.0 reduce-scatter.3.cloned.1.call-update
  110.4 0.2 reduce-scatter.5.cloned.1.call-start
  110.7 0.9 copy-done
  111.5 35.1 %fusion.1 = f32[1,3072,256]{1,2,0:T(8,128)} fusion(f32[3072,1536]{1,0:T(8,128)} %param.4, bf16[1,1536,256]{2,1,0:T(8,128)(2,1)S(1)} %copy-done, f32[3072]{0:T(1024)S(1)} %bitcast.33, f32[1536]{0:T(1024)S(1)} %get-tuple-element.4), kind=kOutput, calls=%fused_computation.2 | convolution fusion | flops 14497087488 | bytes 22824960 | tf_op jit(solution)/shard_map/ij,kjw->kiw/dot_general | solution.py:16
  146.7 0.0 reduce-scatter.5.cloned.1.call-update
  146.7 0.0 all-reduce.4.cloned.1.call-start
  146.7 1.0 constant_dynamic-slice_fusion.1
  147.8 0.0 copy-start.1
  147.8 0.2 copy.10
  148.0 2.9 reduce-scatter.3.cloned.1.call-done
  151.0 1.0 constant_dynamic-update-slice_fusion.1
  152.0 40.8 %reduce-scatter.5.cloned.1.call-done = f32[1,384,256]{1,2,0:T(8,128)} async-done(((f32[1,3072,256]{1,2,0:T(8,128)}), f32[1,384,256]{1,2,0:T(8,128)}) %reduce-scatter.5.cloned.1.call-update) | async-done | bytes 393232 | tf_op jit(solution)/shard_map/reduce_scatter | solution.py:63
  192.8 1.0 constant_dynamic-update-slice_fusion
  193.9 1.9 fusion.10
  195.8 0.0 all-reduce.4.cloned.1.call-update
  195.8 1.1 copy.8
  197.0 129.8 %all-reduce.4.cloned.1.call-done = f32[2,256,256]{2,1,0:T(8,128)} async-done(((f32[2,256,256]{2,1,0:T(8,128)}), f32[2,256,256]{2,1,0:T(8,128)}) %all-reduce.4.cloned.1.call-update) | async-done | bytes 524304 | tf_op jit(solution)/shard_map/psum | solution.py:67
  326.8 0.0 copy-done.1
  326.8 1.9 convert_subtract_fusion
  (3 shorter events, 0.0 us)
Async XLA Ops:
  7.2 3.0 copy-start.2
  7.2 68.0 %all-reduce.6.cloned.1.call-start = ((), (), s32[]{:S(2)}) async-start(), calls=%async_computation.5 | async-start | bytes 3145728 | tf_op jit(solution)/shard_map/psum | solution.py:11
  10.1 140.9 %reduce-scatter.3.cloned.1.call-start = ((), (), s32[]{:S(2)}) async-start(), calls=%async_computation.2 | async-start | bytes 3538944 | tf_op jit(solution)/shard_map/reduce_scatter | solution.py:63
  110.4 1.1 copy-start
  110.4 82.4 %reduce-scatter.5.cloned.1.call-start = ((), (), s32[]{:S(2)}) async-start(), calls=%async_computation.3 | async-start | bytes 3538944 | tf_op jit(solution)/shard_map/reduce_scatter | solution.py:63
  146.7 180.1 %all-reduce.4.cloned.1.call-start = ((), (), s32[]{:S(2)}) async-start(), calls=%async_computation.4 | async-start | bytes 1048576 | tf_op jit(solution)/shard_map/psum | solution.py:67
  147.8 179.0 %copy-start.1 = (bf16[2,256,256]{2,1,0:T(8,128)(2,1)S(1)}, bf16[2,256,256]{2,1,0:T(8,128)(2,1)}, u32[]{:S(2)}) copy-start(bf16[2,256,256]{2,1,0:T(8,128)(2,1)} %param.6) | copy-start | bytes 786436
Sparse Core Ops, SparseCore 0:
  11.7 63.4 all-reduce.5
  110.6 40.3 reduce-scatter.2
  153.3 39.5 reduce-scatter.4
  198.5 128.1 all-reduce.3
where the time goes:
time: 336 us; the launch traced here: 335 us
  waiting for transfers between devices  238 us (71%)
  matrix products  72.3 us (22%)
  between operations  13.9 us (4%)
  local copies, waits for them, and re-layouts  5.6 us (2%)
  other arithmetic  4.8 us (1%)
    psum x1, waiting for transfers between devices, shards(): total = lax.psum(term, ('prow', 'pcol'))  130 us
    dot_general x2, matrix products, multiply(): jnp.einsum('ij,kjw->kiw', ancestor, weighted, precision=lax.Precision.HIG...  70.4 us
    psum x1, waiting for transfers between devices, broadcast(): return lax.psum(jnp.where(mine, shard, jnp.zeros_like(shard)), axis)  64.6 us
    reduce_scatter x2, waiting for transfers between devices, shards(): lax.psum_scatter(negated_one, 'pcol', scatter_dimension=1, tiled=True)  43.8 us
  transfers between devices with their start and end apart: 4, of which 4 were waited for; matrix products, arithmetic and copies ran while one was open for 12% of the time, Pallas kernels for 0%

commit v1 on v0

--- a/solution.py
+++ b/solution.py
@@ -64,7 +64,8 @@
         pieces.append(negated_one)
     column_block = jnp.concatenate(blocks, 0)
     term = reduced_term(own_rows, column_block, column)
-    total = lax.psum(term, ("prow", "pcol"))
+    parts = lax.all_gather(term, ("prow", "pcol"), axis=0, tiled=False)
+    total = parts.sum(axis=0)
     diagonal = inverse_diag.astype(jnp.float32) - total
     return (column_block, diagonal)
 

time: 336 us -> 324 us (0.964)
  waiting for transfers between devices: 238 us -> 221 us
  other arithmetic: 4.8 us -> 10.7 us
    psum x1 -> x0, waiting for transfers between devices: 130 us -> none  [shards(): total = lax.psum(term, ('prow', 'pcol'))]
    all_gather x0 -> x1, waiting for transfers between devices: none -> 113 us  [shards(): parts = lax.all_gather(term, ('prow', 'pcol'), axis=0, tiled=False)]
    reduce_sum x0 -> x1, other arithmetic: none -> 6.93 us  [shards(): total = parts.sum(axis=0)]
where the time goes in v1:
time: 324 us
  waiting for transfers between devices  221 us (68%)
  matrix products  72.3 us (22%)
  between operations  13.9 us (4%)
  other arithmetic  10.7 us (3%)
  local copies, waits for them, and re-layouts  5.6 us (2%)
    all_gather x1, waiting for transfers between devices, shards(): parts = lax.all_gather(term, ('prow', 'pcol'), axis=0, tiled=False)  113 us
    dot_general x2, matrix products, multiply(): jnp.einsum('ij,kjw->kiw', ancestor, weighted, precision=lax.Precision.HIG...  70.4 us
    psum x1, waiting for transfers between devices, broadcast(): return lax.psum(jnp.where(mine, shard, jnp.zeros_like(shard)), axis)  64.6 us
    reduce_scatter x2, waiting for transfers between devices, shards(): lax.psum_scatter(negated_one, 'pcol', scatter_dimension=1, tiled=True)  43.6 us
    reduce_sum x1, other arithmetic, shards(): total = parts.sum(axis=0)  6.93 us
  transfers between devices with their start and end apart: 4, of which 4 were waited for; matrix products, arithmetic and copies ran while one was open for 12% of the time, Pallas kernels for 0%

profile of v1, /device:TPU:0, one launch (start us, length us, event | category | flops | bytes accessed | tf_op | source)
XLA Modules:
  0.0 324.2 jit_solution(7329764280495390541)
XLA Ops:
  7.2 0.0 copy-start.2
  7.2 0.0 all-reduce.3.cloned.1.call-start
  7.2 2.8 dynamic-slice_select_fusion
  10.1 0.0 all-reduce.3.cloned.1.call-update
  10.1 0.0 reduce-scatter.3.cloned.1.call-start
  10.1 0.0 copy-done.2
  10.2 0.1 broadcast_bitcast_fusion
  10.2 0.1 copy.14
  10.3 0.1 dynamic-slice_reduce_fusion
  10.4 0.1 dynamic-slice_negate_fusion
  10.5 64.6 %all-reduce.3.cloned.1.call-done = (bf16[1,1536,256]{2,1,0:T(8,128)(2,1)}, bf16[1,1536,256]{2,1,0:T(8,128)(2,1)}) async-done(((bf16[1,1536,256]{2,1,0:T(8,128)(2,1)}, bf16[1,1536,256]{2,1,0:T(8,128)(2,1)}), (bf16[1,1536,256]{2,1,0:T(8,128)(2,1)}, bf16[1,1536,256]{2,1,0:T(8,128)(2,1)})) %all-reduce.3.cloned.1.call-update) | async-done | bytes 1572880 | tf_op jit(solution)/shard_map/psum | solution.py:11
  75.2 35.3 %fusion.3 = f32[1,3072,256]{1,2,0:T(8,128)} fusion(f32[3072,1536]{1,0:T(8,128)} %param.4, bf16[1,1536,256]{2,1,0:T(8,128)(2,1)} %get-tuple-element.8, f32[3072]{0:T(1024)S(1)} %bitcast.36, f32[1536]{0:T(1024)S(1)} %get-tuple-element.7), kind=kOutput, calls=%fused_computation.5 | convolution fusion | flops 14497087488 | bytes 22824960 | tf_op jit(solution)/shard_map/ij,kjw->kiw/dot_general | solution.py:16
  110.4 0.0 copy-start
  110.4 0.0 reduce-scatter.3.cloned.1.call-update
  110.4 0.2 reduce-scatter.5.cloned.1.call-start
  110.7 0.9 copy-done
  111.5 35.1 %fusion.1 = f32[1,3072,256]{1,2,0:T(8,128)} fusion(f32[3072,1536]{1,0:T(8,128)} %param.4, bf16[1,1536,256]{2,1,0:T(8,128)(2,1)S(1)} %copy-done, f32[3072]{0:T(1024)S(1)} %bitcast.35, f32[1536]{0:T(1024)S(1)} %get-tuple-element.6), kind=kOutput, calls=%fused_computation.2 | convolution fusion | flops 14497087488 | bytes 22824960 | tf_op jit(solution)/shard_map/ij,kjw->kiw/dot_general | solution.py:16
  146.7 0.0 reduce-scatter.5.cloned.1.call-update
  146.7 0.3 all-gather.3.cloned.1.call-start
  147.0 1.0 constant_dynamic-slice_fusion.1
  148.0 0.2 copy.13
  148.2 2.7 reduce-scatter.3.cloned.1.call-done
  151.0 1.0 constant_dynamic-update-slice_fusion.1
  152.0 40.8 %reduce-scatter.5.cloned.1.call-done = f32[1,384,256]{1,2,0:T(8,128)} async-done(((f32[1,3072,256]{1,2,0:T(8,128)}), f32[1,384,256]{1,2,0:T(8,128)}) %reduce-scatter.5.cloned.1.call-update) | async-done | bytes 393232 | tf_op jit(solution)/shard_map/reduce_scatter | solution.py:63
  192.8 1.0 constant_dynamic-update-slice_fusion
  193.9 1.9 fusion.10
  195.8 0.0 all-gather.3.cloned.1.call-update
  195.8 1.1 copy.11
  197.0 112.9 %all-gather.3.cloned.1.call-done = f32[64,256,256]{2,1,0:T(8,128)} async-done(((f32[2,256,256]{2,1,0:T(8,128)}), f32[64,256,256]{2,1,0:T(8,128)}) %all-gather.3.cloned.1.call-update) | async-done | bytes 16777232 | tf_op jit(solution)/shard_map/all_gather | solution.py:67
  309.8 6.9 %reduce_sum.9 = f32[2,256,256]{2,1,0:T(8,128)S(1)} reduce(f32[32,2,256,256]{3,2,1,0:T(8,128)} %bitcast.31, f32[]{:T(128)} %constant.44.clone.1), dimensions={0}, to_apply=%region_4.5 | reduce | flops 4063232 | bytes 17301508 | tf_op jit(solution)/shard_map/reduce_sum | solution.py:68
  316.8 0.0 copy-done.1
  316.8 0.8 convert_subtract_fusion
  (4 shorter events, 0.0 us)
Async XLA Ops:
  7.2 3.0 copy-start.2
  7.2 68.0 %all-reduce.3.cloned.1.call-start = ((), (), s32[]{:S(2)}) async-start(), calls=%async_computation.5 | async-start | bytes 3145728 | tf_op jit(solution)/shard_map/psum | solution.py:11
  10.1 140.9 %reduce-scatter.3.cloned.1.call-start = ((), (), s32[]{:S(2)}) async-start(), calls=%async_computation.2 | async-start | bytes 3538944 | tf_op jit(solution)/shard_map/reduce_scatter | solution.py:63
  110.4 1.1 copy-start
  110.4 82.4 %reduce-scatter.5.cloned.1.call-start = ((), (), s32[]{:S(2)}) async-start(), calls=%async_computation.3 | async-start | bytes 3538944 | tf_op jit(solution)/shard_map/reduce_scatter | solution.py:63
  146.7 163.2 %all-gather.3.cloned.1.call-start = ((), (), s32[]{:S(2)}) async-start(), calls=%async_computation.4 | async-start | bytes 17301504 | tf_op jit(solution)/shard_map/all_gather | solution.py:67
  309.8 6.9 %copy-start.1 = (bf16[2,256,256]{2,1,0:T(8,128)(2,1)S(1)}, bf16[2,256,256]{2,1,0:T(8,128)(2,1)}, u32[]{:S(2)}) copy-start(bf16[2,256,256]{2,1,0:T(8,128)(2,1)} %param.6) | copy-start | bytes 786436
Sparse Core Ops, SparseCore 0:
  11.7 63.4 all-reduce.2
  110.6 40.3 reduce-scatter.2
  153.3 39.5 reduce-scatter.4
  196.3 113.5 all-gather.2
